TPU v7x, 128 devices: a whole 4x4x4 slice. The times are simulated.
128 devices in a mesh: row: 8 (over y, core), col: 16 (over z, x).
Axes of the slice: x: 4, y: 4, z: 4, core: 2. Of those that a mesh axis runs over, the one named last changes fastest.
Arguments:
- latents: bfloat16 [256, 16384], P('col', 'row'), may hold values from -30 to 30
- samples: bfloat16 [256, 65536], P('row', 'col'), may hold values from -30 to 30
- warm_dual: float32 [65536], P('col'), may hold values from -0.6 to 0.6
Outputs:
- targets: bfloat16 [256, 16384], P('col', 'row')
- pot_lat: float32 [16384], P('row')
- pot_tea: float32 [65536], P('col')
All inputs are finite; a program needn't handle non-finite values.
Results may differ from a plain program's by a relative error of at most 0.012.
Values may be sent and summed in bfloat16 or wider, within the bound.
No kernel may reach another device: no remote copies, remote signals or barrier semaphores. Data moves between devices by JAX's collectives and lax.ppermute only.
A program may use at most 192 MiB of HBM per device.

v0:
```python
import math

import jax
import jax.numpy as jnp
from jax import lax
from jax.sharding import PartitionSpec as P

blur_scale = 0.04


def joined(value, axis, join):
    pieces = jax.tree.map(lambda part: lax.all_gather(part, axis), value)
    head = jax.tree.map(lambda part: part[0], pieces)
    tail = jax.tree.map(lambda part: part[1:], pieces)
    running, _ = lax.scan(lambda running, slab: (join(running, slab), None), head, tail)
    return running


def merge_three(earlier, later):
    highest = jnp.maximum(earlier[0], later[0])
    early_factor = jnp.exp(earlier[0] - highest)
    late_factor = jnp.exp(later[0] - highest)
    denominator = earlier[1] * early_factor + later[1] * late_factor
    numerator = earlier[2] * early_factor[None, :] + later[2] * late_factor[None, :]
    return (highest, denominator, numerator)


def across_cols(maxima, totals):
    highest = lax.pmax(maxima, "col")
    summed = lax.psum(totals * jnp.exp(maxima - highest), "col")
    return highest + jnp.log(summed)


def across_rows(maxima, totals):
    highest = lax.pmax(maxima, "row")
    summed = lax.psum(totals * jnp.exp(maxima - highest), "row")
    return highest + jnp.log(summed)


def per_device(latents, samples, warm_dual):
    x_full = lax.all_gather(latents, "col", axis=0, tiled=True)
    y_full = lax.all_gather(samples, "row", axis=0, tiled=True)
    feature_width, row_count = x_full.shape
    col_count = y_full.shape[1]
    latent_count = row_count * lax.axis_size("row")
    teacher_count = col_count * lax.axis_size("col")
    y_norms = jnp.sum(jnp.square(y_full.astype(jnp.float32)), axis=0)
    block_rows = min(512, row_count)
    block_count = row_count // block_rows

    def block_of(index):
        return lax.dynamic_slice_in_dim(x_full, index * block_rows, block_rows, 1)

    def cost_rows(x_cols):
        inner = lax.dot_general(
            x_cols, y_full, (((0,), (0,)), ((), ())), preferred_element_type=jnp.float32
        )
        x_norms = jnp.sum(jnp.square(x_cols.astype(jnp.float32)), axis=0)
        return (x_norms[:, None] + y_norms[None, :] - 2.0 * inner) / (2.0 * feature_width)

    def dual_rows(index):
        scores = (warm_dual[None, :] - cost_rows(block_of(index))) / blur_scale
        maximum = jnp.max(scores, axis=1)
        return (maximum, jnp.sum(jnp.exp(scores - maximum[:, None]), axis=1))

    indices = jnp.arange(block_count, dtype=jnp.int32)
    maxima, totals = lax.map(dual_rows, indices)
    log_total = across_cols(maxima.reshape(row_count), totals.reshape(row_count))
    pot_lat = -blur_scale * (log_total - math.log(teacher_count))

    def dual_cols(index):
        f_rows = lax.dynamic_slice_in_dim(pot_lat, index * block_rows, block_rows, 0)
        scores = (f_rows[:, None] - cost_rows(block_of(index))) / blur_scale
        maximum = jnp.max(scores, axis=0)
        return (maximum, jnp.sum(jnp.exp(scores - maximum[None, :]), axis=0))

    col_maxima, col_totals = lax.map(dual_cols, indices)
    local_high = jnp.max(col_maxima, axis=0)
    local_sum = jnp.sum(col_totals * jnp.exp(col_maxima - local_high[None, :]), axis=0)
    log_cols = across_rows(local_high, local_sum)
    pot_tea = -blur_scale * (log_cols - math.log(latent_count))

    def barycenter(index, carry):
        top_all, den_all, num_all = carry
        scores = (pot_tea[None, :] - cost_rows(block_of(index))) / blur_scale
        block_top = jnp.max(scores, axis=1)
        weights = jnp.exp(scores - block_top[:, None])
        denominator = jnp.sum(weights, axis=1)
        numerator = lax.dot_general(
            y_full,
            weights.astype(jnp.bfloat16),
            (((1,), (1,)), ((), ())),
            preferred_element_type=jnp.float32,
        )
        start = index * block_rows
        top_all = lax.dynamic_update_slice_in_dim(top_all, block_top, start, 0)
        den_all = lax.dynamic_update_slice_in_dim(den_all, denominator, start, 0)
        num_all = lax.dynamic_update_slice_in_dim(num_all, numerator, start, 1)
        return (top_all, den_all, num_all)

    start_carry = (
        jnp.zeros((row_count,), jnp.float32),
        jnp.zeros((row_count,), jnp.float32),
        jnp.zeros((feature_width, row_count), jnp.float32),
    )
    block_top, denominator, numerator = lax.fori_loop(0, block_count, barycenter, start_carry)
    highest, whole_den, whole_num = joined((block_top, denominator, numerator), "col", merge_three)
    share_width = feature_width // lax.axis_size("col")
    offset = lax.axis_index("col") * share_width
    result = lax.dynamic_slice_in_dim(whole_num, offset, share_width, 0) / whole_den[None, :]
    return (result.astype(jnp.bfloat16), pot_lat, pot_tea)


def solution(mesh):
    return jax.shard_map(
        per_device,
        mesh=mesh,
        in_specs=(P("col", "row"), P("row", "col"), P("col")),
        out_specs=(P("col", "row"), P("row"), P("col")),
        check_vma=False,
    )
```

profile of v0, /device:TPU:1, one launch (start us, length us, event | category | flops | bytes accessed | tf_op | source)
XLA Modules:
  0.0 594.7 jit_solution(3918296119347148906)
XLA Ops:
  8.7 29.9 %all-gather.9.cloned.1.call-done = bf16[256,4096]{1,0:T(8,128)(2,1)} async-done(((bf16[32,4096]{1,0:T(8,128)(2,1)}), bf16[256,4096]{1,0:T(8,128)(2,1)}) %all-gather.9.cloned.1.call-update) | async-done | bytes 2097168 | tf_op jit(solution)/shard_map/all_gather | solution.py:42
  38.6 2.0 multiply_reduce_fusion.3
  40.7 40.9 %all-gather.7.cloned.1.call-done = bf16[256,2048]{1,0:T(8,128)(2,1)} async-done(((bf16[16,2048]{1,0:T(8,128)(2,1)}), bf16[256,2048]{1,0:T(8,128)(2,1)}) %all-gather.7.cloned.1.call-update) | async-done | bytes 1048592 | tf_op jit(solution)/shard_map/all_gather | solution.py:41
  81.6 31.2 %while.55 = (s32[]{:T(128)}, f32[4,512]{1,0:T(4,128)S(1)}, f32[4,512]{1,0:T(4,128)S(1)}, f32[4096]{0:T(1024)}, s32[4]{0:T(128)S(1)}, /*index=5*/bf16[256,2048]{1...) while((s32[]{:T(128)}, f32[4,512]{1,0:T(4,128)S(1)}, ...), condition=%wide.region_5.6_spmd, body=%wide.region_1.5_spmd.sunk | while | flops 1093007872 | bytes 19450048 | solution.py:67
  84.0 4.0 fusion.34
  88.0 1.3 exponential_reduce_fusion.4
  91.8 4.0 fusion.34
  95.8 1.3 exponential_reduce_fusion.4
  99.6 4.0 fusion.34
  103.6 1.3 exponential_reduce_fusion.4
  107.5 4.0 fusion.34
  111.5 1.3 exponential_reduce_fusion.4
  112.9 31.4 %pmax.14 = f32[2048]{0:T(1024)S(1)} all-reduce(f32[2048]{0:T(1024)S(1)} %bitcast.58), channel_id=1, replica_groups=mesh['row'=8,'col'=16] {'col'}, use_global_device_ids=true, to_apply=%region_6.7 | all-reduce | flops 2048 | bytes 16384 | tf_op jit(solution)/shard_map/pmax | solution.py:29
  144.3 29.0 %psum.14 = f32[2048]{0:T(1024)S(1)} all-reduce(f32[2048]{0:T(1024)S(1)} %exponential_multiply_fusion.1), channel_id=1, replica_groups=mesh['row'=8,'col'=16] {'col'}, use_global_device_ids=true, to_apply=%region_7.8 | all-reduce | flops 2048 | bytes 16384 | tf_op jit(solution)/shard_map/psum | solution.py:30
  173.3 33.7 %while.56 = (s32[]{:T(128)}, f32[4,4096]{1,0:T(4,128)S(1)}, f32[4,4096]{1,0:T(4,128)S(1)}, s32[4]{0:T(128)S(1)}, f32[2048]{0:T(1024)S(1)}, /*index=5*/bf16[256,2...) while((s32[]{:T(128)}, f32[4,4096]{1,0:T(4,128)S(1)}, ...), condition=%wide.region_12.13_spmd, body=%wide.region_8.12_spmd.sunk | while | flops 1093000704 | bytes 19540164 | solution.py:77
  175.8 4.1 fusion.36
  179.9 1.3 exponential_reduce_fusion.5
  184.3 4.1 fusion.36
  188.4 1.3 exponential_reduce_fusion.5
  192.7 4.1 fusion.36
  196.8 1.3 exponential_reduce_fusion.5
  201.1 4.1 fusion.36
  205.2 1.3 exponential_reduce_fusion.5
  207.1 36.7 %pmax.15 = f32[4096]{0:T(1024)S(1)} all-reduce(f32[4096]{0:T(1024)S(1)} %reduce_max.40), channel_id=1, replica_groups=mesh['row'=8,'col'=16] {'row'}, use_global_device_ids=true, to_apply=%region_14.15 | all-reduce | flops 4096 | bytes 32768 | tf_op jit(solution)/shard_map/pmax | solution.py:35
  243.9 23.7 %psum.15 = f32[4096]{0:T(1024)S(1)} all-reduce(f32[4096]{0:T(1024)S(1)} %exponential_multiply_fusion), channel_id=1, replica_groups=mesh['row'=8,'col'=16] {'row'}, use_global_device_ids=true, to_apply=%region_16.17 | all-reduce | flops 4096 | bytes 32768 | tf_op jit(solution)/shard_map/psum | solution.py:36
  267.9 61.1 %while.57 = (s32[]{:T(128)}, f32[2048]{0:T(1024)S(1)}, f32[2048]{0:T(1024)S(1)}, f32[256,2048]{1,0:T(8,128)S(1)}, f32[4096]{0:T(1024)S(1)}, /*index=5*/bf16[256,...) while((s32[]{:T(128)}, f32[2048]{0:T(1024)S(1)}, ...), condition=%wide.region_21.22_spmd, body=%wide.region_17.21_spmd.sunk | while | flops 2170944000 | bytes 74502376 | solution.py:106
  269.1 4.1 fusion.40
  273.2 3.2 copy-done
  276.4 1.4 fusion.42
  278.1 4.6 fusion.41
  283.2 1.2 multiply_reduce_fusion.10
  284.4 4.1 fusion.40
  288.5 3.2 copy-done
  291.8 1.4 fusion.42
  293.4 4.6 fusion.41
  299.7 4.1 fusion.40
  303.9 3.2 copy-done
  307.1 1.4 fusion.42
  308.7 4.6 fusion.41
  315.0 4.1 fusion.40
  319.1 3.2 copy-done
  322.3 1.4 fusion.42
  324.0 4.6 fusion.41
  329.0 1.3 copy-done.1
  330.4 18.8 %all-gather = f32[32768]{0:T(1024)S(1)} all-gather(f32[2048]{0:T(1024)S(1)} %get-tuple-element.272), channel_id=2, replica_groups=mesh['row'=8,'col'=16] {'col'}, dimensions={0}, use_global_device_ids=true | all-gather | bytes 139264 | tf_op jit(solution)/shard_map/all_gather | solution.py:12
  349.2 19.4 %all-gather.1 = f32[32768]{0:T(1024)S(1)} all-gather(f32[2048]{0:T(1024)S(1)} %get-tuple-element.273), channel_id=3, replica_groups=mesh['row'=8,'col'=16] {'col'}, dimensions={0}, use_global_device_ids=true | all-gather | bytes 139264 | tf_op jit(solution)/shard_map/all_gather | solution.py:12
  368.7 157.7 %all-gather.11.cloned.1.call-done = f32[4096,2048]{1,0:T(8,128)} async-done(((f32[256,2048]{1,0:T(8,128)}), f32[4096,2048]{1,0:T(8,128)}) %all-gather.11.cloned.1.call-update) | async-done | bytes 33554448 | tf_op jit(solution)/shard_map/all_gather | solution.py:12
  526.4 22.3 %slice.35 = f32[3840,2048]{1,0:T(8,128)} slice(f32[4096,2048]{1,0:T(8,128)} %all-gather.11.cloned.1.call-done), slice={[256:4096], [0:2048]} | slice | bytes 62914560 | tf_op jit(solution)/shard_map/slice | solution.py:14
  548.7 38.8 %while.58 = (s32[]{:T(128)}, f32[2048]{0:T(1024)S(1)}, f32[2048]{0:T(1024)S(1)}, f32[256,2048]{1,0:T(8,128)S(1)}, f32[15,2048]{1,0:T(8,128)S(1)}, /*index=5*/f32...) while((s32[]{:T(128)}, f32[2048]{0:T(1024)S(1)}, f32[2048]{0:T(1024)S(1)}, ...), condition=%wide.region_23.24_spmd, body=%wide.region_22.23_spmd.sunk | while | flops 1585154 | bytes 6406237 | solution.py:15
  548.8 2.5 fusion.43
  551.4 2.5 fusion.43
  554.0 2.5 fusion.43
  556.5 2.5 fusion.43
  559.1 2.5 fusion.43
  561.7 2.5 fusion.43
  564.3 2.5 fusion.43
  566.9 2.5 fusion.43
  569.5 2.5 fusion.43
  572.1 2.5 fusion.43
  574.6 2.5 fusion.43
  577.2 2.5 fusion.43
  579.8 2.5 fusion.43
  582.4 2.5 fusion.43
  585.0 2.5 fusion.43
  (134 shorter events, 25.9 us)
Async XLA Ops:
  7.2 31.5 %all-gather.9.cloned.1.call-start = ((), (), s32[]{:S(2)}) async-start(), calls=%async_computation.1 | async-start | bytes 2359296 | tf_op jit(solution)/shard_map/all_gather | solution.py:42
  7.9 73.7 %all-gather.7.cloned.1.call-start = ((), (), s32[]{:S(2)}) async-start(), calls=%async_computation | async-start | bytes 1114112 | tf_op jit(solution)/shard_map/all_gather | solution.py:41
  8.6 517.7 %all-gather.11.cloned.1.call-start = ((), (), s32[]{:S(2)}) async-start(), calls=%async_computation.2 | async-start | bytes 35651584 | tf_op jit(solution)/shard_map/all_gather | solution.py:12
  207.1 60.8 %copy-start.3 = (f32[2048]{0:T(1024)}, f32[2048]{0:T(1024)S(1)}, u32[]{:S(2)}) copy-start(f32[2048]{0:T(1024)S(1)} %get-tuple-element.713) | copy-start | bytes 24580
  267.9 8.5 %copy-start.2 = (bf16[256,4096]{1,0:T(8,128)(2,1)S(1)}, bf16[256,4096]{1,0:T(8,128)(2,1)}, u32[]{:S(2)}) copy-start(bf16[256,4096]{1,0:T(8,128)(2,1)} %get-tuple-element.668) | copy-start | bytes 6291460 | tf_op jit(solution)/shard_map/while
  273.2 3.2 copy-start
  283.2 8.5 %copy-start.2 = (bf16[256,4096]{1,0:T(8,128)(2,1)S(1)}, bf16[256,4096]{1,0:T(8,128)(2,1)}, u32[]{:S(2)}) copy-start(bf16[256,4096]{1,0:T(8,128)(2,1)} %get-tuple-element.668) | copy-start | bytes 6291460 | tf_op jit(solution)/shard_map/while
  288.5 3.2 copy-start
  298.6 8.5 %copy-start.2 = (bf16[256,4096]{1,0:T(8,128)(2,1)S(1)}, bf16[256,4096]{1,0:T(8,128)(2,1)}, u32[]{:S(2)}) copy-start(bf16[256,4096]{1,0:T(8,128)(2,1)} %get-tuple-element.668) | copy-start | bytes 6291460 | tf_op jit(solution)/shard_map/while
  303.8 3.2 copy-start
  313.8 8.5 %copy-start.2 = (bf16[256,4096]{1,0:T(8,128)(2,1)S(1)}, bf16[256,4096]{1,0:T(8,128)(2,1)}, u32[]{:S(2)}) copy-start(bf16[256,4096]{1,0:T(8,128)(2,1)} %get-tuple-element.668) | copy-start | bytes 6291460 | tf_op jit(solution)/shard_map/while
  319.1 3.2 copy-start
  329.0 1.3 copy-start.1
  329.0 219.7 %copy-start.4 = (f32[4096]{0:T(1024)}, f32[4096]{0:T(1024)S(1)}, u32[]{:S(2)}) copy-start(f32[4096]{0:T(1024)S(1)} %get-tuple-element.716) | copy-start | bytes 49156
  526.4 22.3 %slice-start = ((f32[4096,2048]{1,0:T(8,128)}), f32[256,2048]{1,0:T(8,128)S(1)}, s32[]{:S(2)}) async-start(f32[4096,2048]{1,0:T(8,128)} %all-gather.11.cloned.1.call-done), calls=%async_computation.3 | async-start | bytes 4194304 | tf_op jit(solution)/shard_map/slice | solution.py:13
Sparse Core Ops, SparseCore 0:
  9.7 28.8 all-gather.8
  40.8 40.7 all-gather.6
  330.5 195.8 all-gather.10
where the time goes:
time: 596 us; the launch traced here: 595 us
  waiting for transfers between devices  230 us (39%)
  blocking collectives  159 us (27%)
  other arithmetic  82.9 us (14%)
  matrix products  54.3 us (9%)
  local copies, waits for them, and re-layouts  48.1 us (8%)
  between operations  14 us (2%)
  loops' own time  6.46 us (1%)
    all_gather x1, waiting for transfers between devices, joined(): pieces = jax.tree.map(lambda part: lax.all_gather(part, axis), value)  158 us
    dot_general x12, matrix products, cost_rows(): lax.dot_general(x_cols, y_full, (((0,), (0,)), ((), ())), preferred_eleme...  48.8 us
    all_gather x1, waiting for transfers between devices, per_device(): x_full = lax.all_gather(latents, 'col', axis=0, tiled=True)  40.9 us
    all_gather x2, blocking collectives, joined(): pieces = jax.tree.map(lambda part: lax.all_gather(part, axis), value)  38.2 us
    add x15, other arithmetic, merge_three(): earlier[2] * early_factor[None, :] + later[2] * late_factor[None, :]  37.8 us
    pmax x1, blocking collectives, across_rows(): highest = lax.pmax(maxima, 'row')  36.7 us
    pmax x1, blocking collectives, across_cols(): highest = lax.pmax(maxima, 'col')  31.4 us
    all_gather x1, waiting for transfers between devices, per_device(): y_full = lax.all_gather(samples, 'row', axis=0, tiled=True)  29.9 us
  transfers between devices with their start and end apart: 3, of which 3 were waited for; matrix products, arithmetic and copies ran while one was open for 0% of the time, Pallas kernels for 0%

commit v1 on v0

v1 whole, which is shorter than its diff:
```python
import functools
import math

import jax
import jax.numpy as jnp
from jax import lax
from jax.experimental import pallas as pl
from jax.experimental.pallas import tpu as pltpu
from jax.sharding import PartitionSpec as P

BLUR = 0.04
LOG2E = 1.0 / math.log(2.0)
LN2 = math.log(2.0)
LOW, HIGH = 2.0**-90, 2.0**120
CHUNK = 256
TILE = 512
LANES = 128

VMEM = pl.BlockSpec(memory_space=pltpu.VMEM)
SMEM = pl.BlockSpec(memory_space=pltpu.SMEM)
PARAMS = pltpu.CompilerParams(vmem_limit_bytes=48 * 1024 * 1024)


def dot(a, b, ca, cb):
    return lax.dot_general(
        a, b, (((ca,), (cb,)), ((), ())), preferred_element_type=jnp.float32
    )


def place(core_ref, own_ref, sib_ref, y_all):
    core = core_ref[0]
    piece = 32
    for k in range(own_ref.shape[0] // piece):
        rows = slice(k * piece, (k + 1) * piece)
        mine = pl.multiple_of((2 * k + core) * piece, piece)
        other = pl.multiple_of((2 * k + 1 - core) * piece, piece)
        y_all[pl.ds(mine, piece), :] = own_ref[rows, :]
        y_all[pl.ds(other, piece), :] = sib_ref[rows, :]


def square_sums(ref, width):
    parts = []
    for j in range(0, ref.shape[1], width):
        v = ref[:256, j : j + width].astype(jnp.float32)
        parts.append(jnp.sum(v * v, axis=0, keepdims=True))
    return parts


def lse2(stacked):
    top = jnp.max(stacked, axis=0, keepdims=True)
    return top + jnp.log2(jnp.sum(jnp.exp2(stacked - top), axis=0, keepdims=True))


def columns_of(row_ref, col_ref):
    for i in range(0, row_ref.shape[1], LANES):
        block = jnp.broadcast_to(row_ref[0:1, i : i + LANES], (LANES, LANES))
        col_ref[i : i + LANES, :] = block.T


def row_pass(scale, core_ref, x_ref, own_ref, sib_ref, warm_ref, out_ref, yn_ref, y_all, beta, sums, tops):
    rows, cols = x_ref.shape[1], own_ref.shape[1]
    place(core_ref, own_ref, sib_ref, y_all)
    for j, part in enumerate(square_sums(y_all, TILE)):
        sl = slice(j * TILE, (j + 1) * TILE)
        yn_ref[0:1, sl] = part
        beta[0:1, sl] = warm_ref[0:1, sl] * (LOG2E / BLUR) - part * (0.5 * scale)
    sample = dot(x_ref[:, :LANES].T, y_all[:, :TILE], 1, 0) * scale + beta[0:1, :TILE]
    shift = jnp.max(sample)

    def chunk(c, _):
        base = pl.multiple_of(c * CHUNK, CHUNK)
        xt = x_ref[:, pl.ds(base, CHUNK)].T
        acc = None
        for j in range(0, cols, TILE):
            b = beta[0:1, j : j + TILE] - shift
            e = jnp.exp2(dot(xt, y_all[:, j : j + TILE], 1, 0) * scale + b)
            part = e[:, :LANES]
            for k in range(LANES, TILE, LANES):
                part = part + e[:, k : k + LANES]
            acc = part if acc is None else acc + part
        sums[pl.ds(base, CHUNK), :] = acc
        return 0

    lax.fori_loop(0, rows // CHUNK, chunk, 0)
    good = []
    for i in range(0, rows, LANES):
        s = jnp.sum(sums[i : i + LANES, :].T, axis=0, keepdims=True)
        good.append(jnp.where((s > LOW) & (s < HIGH), 1.0, 0.0))
        out_ref[:, i : i + LANES] = jnp.broadcast_to(shift + jnp.log2(s), (out_ref.shape[0], LANES))
    ok = functools.reduce(jnp.minimum, good)

    @pl.when(jnp.min(ok) < 0.5)
    def _():
        def slow(c, _):
            base = pl.multiple_of(c * LANES, LANES)
            xt = x_ref[:, pl.ds(base, LANES)].T

            def tile(j, state):
                top, total = state
                lane = pl.multiple_of(j * LANES, LANES)
                t = dot(xt, y_all[:, pl.ds(lane, LANES)], 1, 0) * scale + beta[0:1, pl.ds(lane, LANES)]
                new = jnp.maximum(top, t)
                return new, total * jnp.exp2(top - new) + jnp.exp2(t - new)

            first = jnp.full((LANES, LANES), -1e30, jnp.float32)
            top, total = lax.fori_loop(0, cols // LANES, tile, (first, jnp.zeros_like(first)))
            top, total = top.T, total.T
            high = jnp.max(top, axis=0, keepdims=True)
            s = jnp.sum(total * jnp.exp2(top - high), axis=0, keepdims=True)
            out_ref[:, pl.ds(base, LANES)] = jnp.broadcast_to(high + jnp.log2(s), (out_ref.shape[0], LANES))
            return 0

        lax.fori_loop(0, rows // LANES, slow, 0)


def col_pass(scale, count, core_ref, x_ref, own_ref, sib_ref, lg_ref, out_ref, l_ref, pot_ref, y_all, x_t, l_col):
    rows, cols = x_ref.shape[1], own_ref.shape[1]
    place(core_ref, own_ref, sib_ref, y_all)
    l_ref[...] = lse2(lg_ref[...])
    columns_of(l_ref, l_col)
    for j, part in enumerate(square_sums(x_ref, TILE)):
        sl = slice(j * TILE, (j + 1) * TILE)
        pot_ref[0:1, sl] = part / 512.0 - (BLUR * LN2) * l_ref[0:1, sl] + BLUR * math.log(count)
    for i in range(0, rows, CHUNK):
        x_t[i : i + CHUNK, :] = x_ref[:, i : i + CHUNK].T
    sample = dot(x_t[:CHUNK, :], y_all[:, :LANES], 1, 0) * scale - l_col[:CHUNK, :]
    shift = jnp.max(sample)

    def tile(j, ok):
        lane = pl.multiple_of(j * TILE, TILE)
        y_tile = y_all[:, pl.ds(lane, TILE)]
        accs = [None] * (TILE // LANES)
        for i in range(0, rows, CHUNK):
            g = dot(x_t[i : i + CHUNK, :], y_tile, 1, 0)
            b = l_col[i : i + CHUNK, :] + shift
            for k in range(TILE // LANES):
                e = jnp.exp2(g[:, k * LANES : (k + 1) * LANES] * scale - b)
                part = jnp.sum(e.reshape(CHUNK // 8, 8, LANES), axis=0)
                accs[k] = part if accs[k] is None else accs[k] + part
        for k in range(TILE // LANES):
            s = jnp.sum(accs[k], axis=0, keepdims=True)
            ok = jnp.minimum(ok, jnp.where((s > LOW) & (s < HIGH), 1.0, 0.0))
            out_ref[:, pl.ds(lane + k * LANES, LANES)] = jnp.broadcast_to(shift + jnp.log2(s), (out_ref.shape[0], LANES))
        return ok

    ok = lax.fori_loop(0, cols // TILE, tile, jnp.ones((1, LANES), jnp.float32))

    @pl.when(jnp.min(ok) < 0.5)
    def _():
        def slow(j, _):
            lane = pl.multiple_of(j * LANES, LANES)
            y_tile = y_all[:, pl.ds(lane, LANES)]

            def rows_of(c, state):
                top, total = state
                base = pl.multiple_of(c * LANES, LANES)
                t = dot(x_t[pl.ds(base, LANES), :], y_tile, 1, 0) * scale - l_col[pl.ds(base, LANES), :]
                new = jnp.maximum(top, t)
                return new, total * jnp.exp2(top - new) + jnp.exp2(t - new)

            first = jnp.full((LANES, LANES), -1e30, jnp.float32)
            top, total = lax.fori_loop(0, rows // LANES, rows_of, (first, jnp.zeros_like(first)))
            high = jnp.max(top, axis=0, keepdims=True)
            s = jnp.sum(total * jnp.exp2(top - high), axis=0, keepdims=True)
            out_ref[:, pl.ds(lane, LANES)] = jnp.broadcast_to(high + jnp.log2(s), (out_ref.shape[0], LANES))
            return 0

        lax.fori_loop(0, cols // LANES, slow, 0)


def mean_pass(scale, ratio, count, core_ref, x_ref, own_ref, sib_ref, mg_ref, l_ref, yn_ref, out_ref, pot_ref, y_all, l_col, bias, w_even, w_odd, den):
    rows, cols = x_ref.shape[1], own_ref.shape[1]
    features = x_ref.shape[0]
    place(core_ref, own_ref, sib_ref, y_all)
    y_all[features:, :] = jnp.ones((y_all.shape[0] - features, cols), y_all.dtype)
    m = lse2(mg_ref[...])
    pot_ref[...] = yn_ref[...] / 512.0 - (BLUR * LN2) * (m + ratio)
    bias[...] = math.log2(count) - m
    columns_of(l_ref, l_col)

    def weigh(c, w):
        base = pl.multiple_of(c * CHUNK, CHUNK)
        xt = x_ref[:, pl.ds(base, CHUNK)].T
        lc = l_col[pl.ds(base, CHUNK), :]
        for j in range(0, cols, TILE):
            g = dot(xt, y_all[:features, j : j + TILE], 1, 0)
            for k in range(0, TILE, LANES):
                t = g[:, k : k + LANES] * scale + (bias[0:1, j + k : j + k + LANES] - lc)
                w[:, j + k : j + k + LANES] = jnp.exp2(t).astype(jnp.bfloat16)

    def gather(c, w):
        base = pl.multiple_of(c * CHUNK, CHUNK)
        num = dot(y_all[...], w[...], 1, 1)
        out_ref[:, pl.ds(base, CHUNK)] = num[:features].astype(jnp.bfloat16)
        den[0:1, pl.ds(base, CHUNK)] = num[features : features + 1]

    last = rows // CHUNK - 1
    weigh(0, w_even)

    def pair(h, _):
        c = 2 * h
        weigh(c + 1, w_odd)
        gather(c, w_even)
        weigh(jnp.minimum(c + 2, last), w_even)
        gather(c + 1, w_odd)
        return 0

    lax.fori_loop(0, rows // CHUNK // 2, pair, 0)
    share = out_ref.shape[0] // 16
    width = rows // 8
    high = den[...].astype(jnp.bfloat16).astype(jnp.float32)
    low = den[...] - high
    grid = jnp.concatenate(
        [v[0:1, k * width : (k + 1) * width] for v in (high, low) for k in range(8)], axis=0
    ).astype(jnp.bfloat16)
    for k in range(out_ref.shape[0] // share):
        out_ref[k * share : (k + 1) * share, rows : rows + width] = grid


def finish(rows, in_ref, out_ref):
    share = out_ref.shape[0]
    width = rows // 8
    total = None
    for k in range(in_ref.shape[0] // share):
        part = in_ref[k * share : (k + 1) * share, :].astype(jnp.float32)
        total = part if total is None else total + part
    den = total[:8, rows:] + total[8:16, rows:]
    for k in range(8):
        sl = slice(k * width, (k + 1) * width)
        out_ref[:, sl] = (total[:, sl] / den[k : k + 1, :]).astype(jnp.bfloat16)


def per_device(latents, samples, warm_dual):
    n_row, n_col = lax.axis_size("row"), lax.axis_size("col")
    rows, cols = latents.shape[1], samples.shape[1]
    features = latents.shape[0] * n_col
    all_rows, all_cols = rows * n_row, cols * n_col
    scale = 2.0 * LOG2E / (2.0 * features * BLUR)
    f32, b16 = jnp.float32, jnp.bfloat16
    core = (lax.axis_index("row") % 2).astype(jnp.int32).reshape(1)

    def spread(v, axis, n, **kw):
        return lax.all_to_all(jnp.tile(v, (n, 1)), axis, 0, 0, tiled=True, **kw)

    groups = [[2 * k + c for k in range(n_row // 2)] for c in range(2)]
    own = spread(samples, "row", n_row // 2, axis_index_groups=groups)
    x = spread(latents, "col", n_col)
    sib = lax.ppermute(own, "row", [(s, s ^ 1) for s in range(n_row)])

    y_scratch = pltpu.VMEM((features, cols), b16)
    l_part, yn = pl.pallas_call(
        functools.partial(row_pass, scale),
        out_shape=[jax.ShapeDtypeStruct((n_col, rows), f32), jax.ShapeDtypeStruct((1, cols), f32)],
        in_specs=[SMEM, VMEM, VMEM, VMEM, VMEM],
        out_specs=[VMEM, VMEM],
        scratch_shapes=[y_scratch, pltpu.VMEM((1, cols), f32), pltpu.VMEM((rows, LANES), f32), pltpu.VMEM((rows, LANES), f32)],
        compiler_params=PARAMS,
        name="row_pass",
    )(core, x, own, sib, warm_dual.reshape(1, cols))
    l_all = lax.all_to_all(l_part, "col", 0, 0, tiled=True)
    m_part, l_sum, pot_lat = pl.pallas_call(
        functools.partial(col_pass, scale, all_cols),
        out_shape=[jax.ShapeDtypeStruct((n_row, cols), f32), jax.ShapeDtypeStruct((1, rows), f32), jax.ShapeDtypeStruct((1, rows), f32)],
        in_specs=[SMEM, VMEM, VMEM, VMEM, VMEM],
        out_specs=[VMEM, VMEM, VMEM],
        scratch_shapes=[y_scratch, pltpu.VMEM((rows, features), b16), pltpu.VMEM((rows, LANES), f32)],
        compiler_params=PARAMS,
        name="col_pass",
    )(core, x, own, sib, l_all)
    m_all = lax.all_to_all(m_part, "row", 0, 0, tiled=True)
    num, pot_tea = pl.pallas_call(
        functools.partial(mean_pass, scale, math.log2(all_cols / all_rows), all_rows),
        out_shape=[jax.ShapeDtypeStruct((features, rows + rows // 8), b16), jax.ShapeDtypeStruct((1, cols), f32)],
        in_specs=[SMEM, VMEM, VMEM, VMEM, VMEM, VMEM, VMEM],
        out_specs=[VMEM, VMEM],
        scratch_shapes=[
            pltpu.VMEM((features + 16, cols), b16),
            pltpu.VMEM((rows, LANES), f32),
            pltpu.VMEM((1, cols), f32),
            pltpu.VMEM((CHUNK, cols), b16),
            pltpu.VMEM((CHUNK, cols), b16),
            pltpu.VMEM((1, rows), f32),
        ],
        compiler_params=PARAMS,
        name="mean_pass",
    )(core, x, own, sib, m_all, l_sum, yn)
    got = lax.all_to_all(num, "col", 0, 0, tiled=True)
    targets = pl.pallas_call(
        functools.partial(finish, rows),
        out_shape=jax.ShapeDtypeStruct((features // n_col, rows), b16),
        in_specs=[VMEM],
        out_specs=VMEM,
        name="finish",
    )(got)
    return targets, pot_lat.reshape(rows), pot_tea.reshape(cols)


def solution(mesh):
    return jax.shard_map(
        per_device,
        mesh=mesh,
        in_specs=(P("col", "row"), P("row", "col"), P("col")),
        out_specs=(P("col", "row"), P("row"), P("col")),
        check_vma=False,
    )
```

time: 596 us -> 211 us (0.35)
  waiting for transfers between devices: 230 us -> 17.4 us
  Pallas kernels: 0 us -> 119 us
  blocking collectives: 159 us -> 60 us
  other arithmetic: 82.9 us -> 0 us
  matrix products: 54.3 us -> 0 us
  local copies, waits for them, and re-layouts: 48.1 us -> 2.54 us
  between operations: 14 us -> 0.7 us
  starting transfers between devices: 0.11 us -> 9.54 us
  loops' own time: 6.46 us -> 0 us
    all_gather x3 -> x0, waiting for transfers between devices: 229 us -> none  [the longest x1 158 us: joined(): pieces = jax.tree.map(lambda part: lax.all_gather(part, axis), value)]
    pallas_call x0 -> x4, Pallas kernels: none -> 119 us  [the longest x1 97.3 us: per_device(): pl.pallas_call(functools.partial(col_pass, scale, all_cols), out_shape=[j...]
    pmax x2 -> x0, blocking collectives: 68 us -> none  [the longest x1 36.7 us: across_rows(): highest = lax.pmax(maxima, 'row')]
    all_to_all x0 -> x4, blocking collectives: none -> 60 us  [the longest x1 20.8 us: per_device(): got = lax.all_to_all(num, 'col', 0, 0, tiled=True)]
    dot_general x16 -> x0, matrix products: 54.3 us -> none  [the longest x12 48.8 us: cost_rows(): lax.dot_general(x_cols, y_full, (((0,), (0,)), ((), ())), preferred_eleme...]
    psum x2 -> x0, blocking collectives: 52.8 us -> none  [the longest x1 29 us: across_cols(): summed = lax.psum(totals * jnp.exp(maxima - highest), 'col')]
    reduce_sum x26 -> x0, other arithmetic: 44.1 us -> none  [the longest x4 18.5 us: barycenter(): denominator = jnp.sum(weights, axis=1)]
    all_gather x2 -> x0, blocking collectives: 38.2 us -> none  [joined(): pieces = jax.tree.map(lambda part: lax.all_gather(part, axis), value)]
  transfers between devices with their start and end apart: 3 -> 2, of which waited for: 3 -> 1; matrix products, arithmetic and copies ran while one was open for 0% -> 1% of each run, Pallas kernels for 0% -> 0%
where the time goes in v1:
time: 211 us; the launch traced here: 209 us
  Pallas kernels  119 us (56%)
  blocking collectives  60 us (28%)
  waiting for transfers between devices  17.4 us (8%)
  starting transfers between devices  9.54 us (5%)
  local copies, waits for them, and re-layouts  2.54 us (1%)
    pallas_call x1, Pallas kernels, per_device(): pl.pallas_call(functools.partial(col_pass, scale, all_cols), out_shape=[j...  97.3 us
    all_to_all x1, blocking collectives, per_device(): got = lax.all_to_all(num, 'col', 0, 0, tiled=True)  20.8 us
    all_to_all x1, blocking collectives, spread(): return lax.all_to_all(jnp.tile(v, (n, 1)), axis, 0, 0, tiled=True, **kw)  19.2 us
    all_to_all x1, waiting for transfers between devices, spread(): return lax.all_to_all(jnp.tile(v, (n, 1)), axis, 0, 0, tiled=True, **kw)  17.4 us
    pallas_call x1, Pallas kernels, per_device(): pl.pallas_call(functools.partial(mean_pass, scale, math.log2(all_cols / a...  12.5 us
    all_to_all x1, blocking collectives, per_device(): l_all = lax.all_to_all(l_part, 'col', 0, 0, tiled=True)  10.5 us
    all_to_all x1, blocking collectives, per_device(): m_all = lax.all_to_all(m_part, 'row', 0, 0, tiled=True)  9.52 us
    all_to_all x1, starting transfers between devices, spread(): return lax.all_to_all(jnp.tile(v, (n, 1)), axis, 0, 0, tiled=True, **kw)  7.73 us
  transfers between devices with their start and end apart: 2, of which 1 were waited for; matrix products, arithmetic and copies ran while one was open for 1% of the time, Pallas kernels for 0%

profile of v1, /device:TPU:1, one launch (start us, length us, event | category | flops | bytes accessed | tf_op | source)
XLA Modules:
  0.0 209.5 jit_solution(6830084283777929361)
XLA Ops:
  0.6 1.0 tile.5
  1.7 0.0 copy-start.1
  1.7 19.2 %all_to_all.49 = bf16[4,32,4096]{2,1,0:T(8,128)(2,1)S(1)} all-to-all(bf16[4,32,4096]{2,1,0:T(8,128)(2,1)S(1)} %tile.5), channel_id=1, replica_groups={{0,32,64,96},{16,48,80,112},{1,33,65,97},{17,49,81,113},{2,34,66,98},{1..., dimensions={0} | all-to-all | bytes 2097152 | tf_op jit(solution)/shard_map/all_to_all | solution.py:243
  20.9 1.8 collective-permute-start
  22.7 0.0 copy-done.1
  22.7 1.1 tile.4
  23.8 0.0 copy-start
  23.8 7.7 %all-to-all-start = ((bf16[16,16,2048]{2,1,0:T(8,128)(2,1)}), bf16[16,16,2048]{2,1,0:T(8,128)(2,1)S(1)}, u32[]{:S(2)}, u32[]{:S(2)}) async-start(bf16[16,16,2048]{2,1,0:T(8,128)(2,1)} %tile.4), calls=%async_computation | async-start | bytes 2097152 | tf_op jit(solution)/shard_map/all_to_all | solution.py:243
  31.5 17.4 %all-to-all-done = bf16[16,16,2048]{2,1,0:T(8,128)(2,1)S(1)} async-done(((bf16[16,16,2048]{2,1,0:T(8,128)(2,1)}), bf16[16,16,2048]{2,1,0:T(8,128)(2,1)S(1)}, u32[]{:S(2)}, u32[]{:S(2)}) %all-to-all-start) | async-done | bytes 1048608 | tf_op jit(solution)/shard_map/all_to_all | solution.py:243
  48.9 0.0 collective-permute-done.sib_ref
  48.9 0.0 copy-done
  48.9 7.5 %row_pass.1 = (f32[16,2048]{1,0:T(8,128)S(1)}, f32[1,4096]{1,0:T(1,128)S(1)}) custom-call(s32[1]{0:T(128)} %bitcast.core_ref, bf16[256,2048]{1,0:T(8,128)(2,1)S(1)} %bitcast.20, bf16[128,4096]{1,0:T(8,128)(2,1)S(1)} %bitcast.17, bf16[128,4096]{1,0:T(8,128)(2,1)S(1)} %collective-permute-done.sib_ref, f32[1,4096]{1,0:T(1,128)S(1)} %bitcast.28), custom_call_target="tpu_custom_call" | custom-call | tf_op jit(solution)/shard_map/row_pass/pallas_call | solution.py:251
  56.4 0.1 copy.6
  56.5 10.5 %all_to_all.50 = f32[16,1,2048]{2,1,0:T(1,128)S(1)} all-to-all(f32[16,1,2048]{2,1,0:T(1,128)S(1)} %copy.6), channel_id=1, replica_groups=mesh['row'=8,'col'=16] {'col'}, dimensions={0} | all-to-all | bytes 262144 | tf_op jit(solution)/shard_map/all_to_all | solution.py:260
  67.0 97.3 %col_pass.1 = (f32[8,4096]{1,0:T(8,128)S(1)}, f32[1,2048]{1,0:T(1,128)S(1)}, f32[1,2048]{1,0:T(1,128)}) custom-call(s32[1]{0:T(128)} %bitcast.core_ref, bf16[256,2048]{1,0:T(8,128)(2,1)S(1)} %bitcast.21, bf16[128,4096]{1,0:T(8,128)(2,1)S(1)} %bitcast.18, bf16[128,4096]{1,0:T(8,128)(2,1)S(1)} %collective-permute-done.sib_ref, f32[16,2048]{1,0:T(8,128)S(1)} %bitcast.25), custom_call_target="tpu_custom_call" | custom-call | tf_op jit(solution)/shard_map/col_pass/pallas_call | solution.py:261
  164.4 0.1 copy.7
  164.5 9.5 %all_to_all.51 = f32[8,1,4096]{2,1,0:T(1,128)S(1)} all-to-all(f32[8,1,4096]{2,1,0:T(1,128)S(1)} %copy.7), channel_id=1, replica_groups=mesh['row'=8,'col'=16] {'row'}, dimensions={0} | all-to-all | bytes 262144 | tf_op jit(solution)/shard_map/all_to_all | solution.py:270
  174.0 0.1 copy.12
  174.1 12.5 %mean_pass.1 = (bf16[256,2304]{1,0:T(8,128)(2,1)S(1)}, f32[1,4096]{1,0:T(1,128)}) custom-call(s32[1]{0:T(128)} %bitcast.core_ref, bf16[256,2048]{1,0:T(8,128)(2,1)S(1)} %bitcast.22, bf16[128,4096]{1,0:T(8,128)(2,1)S(1)} %bitcast.19, bf16[128,4096]{1,0:T(8,128)(2,1)S(1)} %collective-permute-done.sib_ref, f32[8,4096]{1,0:T(8,128)S(1)} %bitcast.24, ...), custom_call_target="tpu_custom_call" | custom-call | tf_op jit(solution)/shard_map/mean_pass/pallas_call | solution.py:271
  186.6 20.8 %all_to_all.52 = bf16[16,16,2304]{2,1,0:T(8,128)(2,1)} all-to-all(bf16[16,16,2304]{2,1,0:T(8,128)(2,1)S(1)} %bitcast.23), channel_id=1, replica_groups=mesh['row'=8,'col'=16] {'col'}, dimensions={0} | all-to-all | bytes 2359296 | tf_op jit(solution)/shard_map/all_to_all | solution.py:287
  207.4 2.1 finish.1
  (1 shorter events, 0.0 us)
Async XLA Ops:
  1.7 21.0 %copy-start.1 = (bf16[16,2048]{1,0:T(8,128)(2,1)S(1)}, bf16[16,2048]{1,0:T(8,128)(2,1)}, u32[]{:S(2)}) copy-start(bf16[16,2048]{1,0:T(8,128)(2,1)} %param.3) | copy-start | bytes 196612
  20.9 28.0 %collective-permute-start = (bf16[128,4096]{1,0:T(8,128)(2,1)S(1)}, bf16[128,4096]{1,0:T(8,128)(2,1)S(1)}, u32[]{:S(2)}, u32[]{:S(2)}) collective-permute-start(bf16[128,4096]{1,0:T(8,128)(2,1)S(1)} %bitcast.16), channel_id=1, source_target_pairs={{0,16},{16,0},{32,48},{48,32},{64,80},{80,64},{96,112},{112,96},{1... | collective-permute-start | bytes 3145736 | tf_op jit(solution)/shard_map/ppermute | solution.py:248
  23.8 25.1 %copy-start = (f32[4096]{0:T(1024)S(1)}, f32[4096]{0:T(1024)}, u32[]{:S(2)}) copy-start(f32[4096]{0:T(1024)} %param.5) | copy-start | bytes 49156
  23.8 25.1 %all-to-all-start = ((bf16[16,16,2048]{2,1,0:T(8,128)(2,1)}), bf16[16,16,2048]{2,1,0:T(8,128)(2,1)S(1)}, u32[]{:S(2)}, u32[]{:S(2)}) async-start(bf16[16,16,2048]{2,1,0:T(8,128)(2,1)} %tile.4), calls=%async_computation | async-start | bytes 2097152 | tf_op jit(solution)/shard_map/all_to_all | solution.py:243
